TPU v7x, 512 devices: a whole 4x4x16 slice. The times are simulated.
512 devices in a mesh: rep: 16 (over x, z_lo), mp: 32 (over z_hi, y, core).
Axes of the slice: x: 4, y: 4, z: 16 (z_hi: 4, z_lo: 4; z = z_hi * 4 + z_lo), core: 2. Of those that a mesh axis runs over, the one named last changes fastest.
Arguments:
- dense_feats: bfloat16 [65536, 13], P(('rep', 'mp')), may hold values from -6 to 6
- bag_counts: int32 [65536, 32, 64], P('rep', 'mp'), may hold values from 0 to 2
- emb_rows: bfloat16 [32, 64, 256], P('mp'), may hold values from -0.625 to 0.625
- v_emb: bfloat16 [8192, 256], P('mp'), may hold values from -0.0625 to 0.0625
- u_emb: bfloat16 [256, 8192], P(None, 'mp'), may hold values from -0.375 to 0.375
- b_emb: bfloat16 [8192], P('mp'), may hold values from -3 to 3
- v_bot: bfloat16 [256, 256], replicated, may hold values from -0.375 to 0.375
- u_bot: bfloat16 [256, 256], replicated, may hold values from -0.375 to 0.375
- b_bot: bfloat16 [256], replicated, may hold values from -3 to 3
- w_first: bfloat16 [13, 1024], replicated, may hold values from -1.75 to 1.75
- b_first: bfloat16 [1024], replicated, may hold values from -3 to 3
- w_second: bfloat16 [1024, 256], replicated, may hold values from -0.1875 to 0.1875
- b_second: bfloat16 [256], replicated, may hold values from -3 to 3
- cot_cross: bfloat16 [65536, 8192], P(('rep', 'mp')), may hold values from -24 to 24
- cot_bottom: bfloat16 [65536, 256], P(('rep', 'mp')), may hold values from -6 to 6
Outputs:
- cross_emb: bfloat16 [65536, 8192], P(('rep', 'mp'))
- cross_bot: bfloat16 [65536, 256], P(('rep', 'mp'))
- grad_table: bfloat16 [32, 64, 256], P('mp')
- grad_v_emb: bfloat16 [8192, 256], P('mp')
- grad_u_emb: bfloat16 [256, 8192], P(None, 'mp')
- grad_b_emb: bfloat16 [8192], P('mp')
- grad_v_bot: bfloat16 [256, 256], replicated
- grad_u_bot: bfloat16 [256, 256], replicated
- grad_b_bot: bfloat16 [256], replicated
- grad_w_first: bfloat16 [13, 1024], replicated
- grad_b_first: bfloat16 [1024], replicated
- grad_w_second: bfloat16 [1024, 256], replicated
- grad_b_second: bfloat16 [256], replicated
Inputs may be any that keep to these rules, and one draw needn't show every extreme that they name: bag_counts[s, t, j] is how often row j of table t occurs in the bag of sample s.
All inputs are finite; a program needn't handle non-finite values.
Results may differ from a plain program's by a relative error of at most 0.029.
Values may be sent and summed in bfloat16 or wider, within the bound.
A program may use at most 64 MiB of HBM per device.

v0:
```python
import math
import jax
import jax.numpy as jnp
from jax import lax
from jax.sharding import PartitionSpec as P


def silu_slope(inputs):
    gate_value = jax.nn.sigmoid(inputs)
    return gate_value * (1.0 + inputs * (1.0 - gate_value))


def contract_rows(left_side, right_side):
    return lax.dot_general(
        left_side, right_side, (((0,), (0,)), ((), ())), preferred_element_type=jnp.float32
    )


def contract_cols(left_side, right_side):
    return lax.dot_general(
        left_side, right_side, (((1,), (1,)), ((), ())), preferred_element_type=jnp.float32
    )


def local(
    dense_feats,
    bag_counts,
    emb_rows,
    v_emb,
    u_emb,
    b_emb,
    v_bot,
    u_bot,
    b_bot,
    w_first,
    b_first,
    w_second,
    b_second,
    cot_cross,
    cot_bottom,
):
    tables = lax.axis_size("mp")
    replicas = lax.axis_size("rep")
    own_rows = dense_feats.shape[0]
    table_rows, width = emb_rows.shape[1:]
    rank = v_emb.shape[1]
    share = width // replicas
    grad_scale = 1.0 / math.sqrt(own_rows * tables * replicas)
    first = lax.axis_index("rep") * share
    pad = -(table_rows + 1) % 128
    packed = jnp.concatenate(
        [v_emb, u_emb.T, emb_rows[0].T, b_emb[:, None], jnp.zeros((width, pad), jnp.bfloat16)],
        axis=1,
    )
    packed = lax.dynamic_slice_in_dim(packed, first, share, 0)
    packed = lax.all_gather(packed, ("mp", "rep"), axis=0, tiled=True)
    counts = bag_counts[:, 0, :].astype(jnp.bfloat16)
    counts = jnp.swapaxes(counts.reshape(tables, own_rows, table_rows), 1, 2)
    counts = lax.all_to_all(counts, "mp", split_axis=0, concat_axis=0, tiled=True)
    first_pre = jnp.dot(dense_feats, w_first, preferred_element_type=jnp.float32) + b_first.astype(
        jnp.float32
    )
    first_act = jax.nn.silu(first_pre).astype(jnp.bfloat16)
    second_pre = jnp.dot(first_act, w_second, preferred_element_type=jnp.float32) + b_second.astype(
        jnp.float32
    )
    bottom = jax.nn.silu(second_pre).astype(jnp.bfloat16)
    v_all = packed[:, :rank]
    u_all = packed[:, rank : 2 * rank]
    emb_all = packed[:, 2 * rank : 2 * rank + table_rows].reshape(tables, width, table_rows)
    b_all = packed[:, 2 * rank + table_rows].reshape(1, tables * width).astype(jnp.float32)
    pooled = lax.dot_general(
        counts, emb_all, (((1,), (2,)), ((0,), (0,))), preferred_element_type=jnp.float32
    ).astype(jnp.bfloat16)
    pooled = jnp.swapaxes(pooled, 0, 1).reshape(own_rows, tables * width)
    low_rank = (
        jnp.dot(pooled, v_all, preferred_element_type=jnp.float32)
        + jnp.dot(bottom, v_bot, preferred_element_type=jnp.float32)
    ).astype(jnp.bfloat16)
    lift_emb = contract_cols(low_rank, u_all) + b_all
    pooled_full = pooled.astype(jnp.float32)
    cross_emb = (pooled_full * (lift_emb + 1.0)).astype(jnp.bfloat16)
    lift_bottom = jnp.dot(low_rank, u_bot, preferred_element_type=jnp.float32) + b_bot.astype(
        jnp.float32
    )
    bottom_full = bottom.astype(jnp.float32)
    cross_bot = (bottom_full * (lift_bottom + 1.0)).astype(jnp.bfloat16)
    cot_rows = cot_cross.astype(jnp.float32)
    d_lift = cot_rows * pooled_full
    d_lift_round = d_lift.astype(jnp.bfloat16)
    cot_low = cot_bottom.astype(jnp.float32)
    d_bottom_lift = cot_low * bottom_full
    d_bottom_round = d_bottom_lift.astype(jnp.bfloat16)
    d_low = (
        jnp.dot(d_lift_round, u_all, preferred_element_type=jnp.float32)
        + contract_cols(d_bottom_round, u_bot)
    ).astype(jnp.bfloat16)
    d_pooled = (cot_rows * (lift_emb + 1.0) + contract_cols(d_low, v_all)).astype(jnp.bfloat16)
    d_tables = jnp.swapaxes(d_pooled.reshape(own_rows, tables, width), 0, 1)
    grad_table = lax.dot_general(
        d_tables, counts, (((1,), (2,)), ((0,), (0,))), preferred_element_type=jnp.float32
    ).reshape(tables * width, table_rows)
    grad_v = contract_rows(pooled, d_low)
    grad_u = contract_rows(d_lift_round, low_rank)
    grad_b = jnp.sum(d_lift, axis=0)
    grads = jnp.concatenate(
        [
            grad_v.astype(jnp.bfloat16),
            grad_u.astype(jnp.bfloat16),
            grad_table.astype(jnp.bfloat16),
            grad_b.astype(jnp.bfloat16)[:, None],
            jnp.zeros((tables * width, pad), jnp.bfloat16),
        ],
        axis=1,
    )
    columns = grads.shape[1]
    grads = jnp.swapaxes(grads.reshape(tables, replicas, share, columns), 0, 1)
    grads = lax.psum_scatter(
        grads.reshape(replicas * tables * share, columns), "rep", scatter_dimension=0, tiled=True
    )
    grads = lax.psum_scatter(
        grads.astype(jnp.float32) * grad_scale, "mp", scatter_dimension=0, tiled=True
    )
    grads = lax.optimization_barrier(grads).astype(jnp.bfloat16)
    grads = lax.all_gather(grads, "rep", axis=0, tiled=True)
    d_bottom = cot_low * (lift_bottom + 1.0) + contract_cols(d_low, v_bot)
    grad_vb = grad_scale * contract_rows(bottom, d_low)
    grad_ub = grad_scale * contract_rows(low_rank, d_bottom_round)
    grad_bb = grad_scale * jnp.sum(d_bottom_lift, axis=0)
    d_second = d_bottom * silu_slope(second_pre)
    d_second_round = d_second.astype(jnp.bfloat16)
    grad_ws = grad_scale * contract_rows(first_act, d_second_round)
    grad_bs = grad_scale * jnp.sum(d_second, axis=0)
    d_first = contract_cols(d_second_round, w_second) * silu_slope(first_pre)
    d_first_round = d_first.astype(jnp.bfloat16)
    grad_wf = grad_scale * contract_rows(dense_feats, d_first_round)
    grad_bf = grad_scale * jnp.sum(d_first, axis=0)
    dense_sums = lax.psum(
        (grad_wf, grad_bf, grad_ws, grad_bs, grad_vb, grad_ub, grad_bb), ("rep", "mp")
    )
    return (
        cross_emb,
        cross_bot,
        grads[:, 2 * rank : 2 * rank + table_rows].T[None],
        grads[:, :rank],
        grads[:, rank : 2 * rank].T,
        grads[:, 2 * rank + table_rows],
        dense_sums[4].astype(jnp.bfloat16),
        dense_sums[5].astype(jnp.bfloat16),
        dense_sums[6].astype(jnp.bfloat16),
        dense_sums[0].astype(jnp.bfloat16),
        dense_sums[1].astype(jnp.bfloat16),
        dense_sums[2].astype(jnp.bfloat16),
        dense_sums[3].astype(jnp.bfloat16),
    )


def solution(mesh):
    return jax.shard_map(
        local,
        mesh=mesh,
        in_specs=(
            P(("rep", "mp"), None),
            P("rep", "mp", None),
            P("mp", None, None),
            P("mp", None),
            P(None, "mp"),
            P("mp"),
            P(),
            P(),
            P(),
            P(),
            P(),
            P(),
            P(),
            P(("rep", "mp"), None),
            P(("rep", "mp"), None),
        ),
        out_specs=(
            P(("rep", "mp"), None),
            P(("rep", "mp"), None),
            P("mp", None, None),
            P("mp", None),
            P(None, "mp"),
            P("mp"),
            P(),
            P(),
            P(),
            P(),
            P(),
            P(),
            P(),
        ),
        check_vma=False,
    )
```

profile of v0, /device:TPU:8, one launch (start us, length us, event | category | flops | bytes accessed | tf_op | source)
XLA Modules:
  0.0 1927.5 jit_solution(6832458507843473368)
XLA Ops:
  14.2 18.3 all-to-all-start
  33.7 1.5 fusion.23
  35.2 1388.3 %all-gather.2.cloned.1.call-done = bf16[8192,640]{1,0:T(8,128)(2,1)} async-done(((bf16[16,640]{1,0:T(8,128)(2,1)}), bf16[8192,640]{1,0:T(8,128)(2,1)}) %all-gather.2.cloned.1.call-update) | async-done | bytes 10485776 | tf_op jit(solution)/shard_map/all_gather | solution.py:56
  1423.6 1.6 slice-done.3
  1425.2 2.0 convolution_convert_fusion.2
  1427.2 2.9 copy.78
  1430.1 3.8 fusion.9
  1434.1 3.4 convolution_convert_fusion
  1437.6 4.0 fusion.5
  1441.8 3.3 convolution_convert_fusion.1
  1445.1 1.4 convert_reduce_fusion
  1446.5 3.0 fusion.3
  1449.5 1.6 fusion.1
  1451.5 1.8 copy.80
  1453.3 2.1 copy.83
  1455.6 4.2 copy.84
  1459.8 4.8 copy.82
  1464.6 2.5 copy.81
  1467.2 1.7 broadcast_in_dim.18
  1468.9 18.8 concatenate.14
  1489.1 265.8 %reduce-scatter.3.cloned.1.call-done = bf16[512,640]{1,0:T(8,128)(2,1)} async-done(((bf16[8192,640]{1,0:T(8,128)(2,1)}), bf16[512,640]{1,0:T(8,128)(2,1)}) %reduce-scatter.3.cloned.1.call-update) | async-done | bytes 655376 | tf_op jit(solution)/shard_map/reduce_scatter | solution.py:118
  1754.9 2.3 convert_multiply_fusion.3
  1758.8 114.1 %all-reduce.2 = (bf16[256,256]{1,0:T(8,128)(2,1)}, bf16[256,256]{1,0:T(8,128)(2,1)}, bf16[256]{0:T(256)(128)(2,1)}, bf16[13,1024]{1,0:T(8,128)(2,1)}, bf16[1024]...) all-reduce(f32[256,256]{1,0:T(8,128)S(1)} %convolution_multiply_fus, ...), channel_id=1, replica_groups=mesh['rep'=16,'mp'=32] {'rep','mp'}, use_global_device_ids=true, to_apply=%region_3.4 | all-reduce | flops 408064 | bytes 2448384 | tf_op jit(solution)/shard_map/psum | solution.py:138
  1873.7 44.4 %all_gather.7 = bf16[256,640]{1,0:T(8,128)(2,1)S(1)} all-gather(bf16[16,640]{1,0:T(8,128)(2,1)S(1)} %convert_element_type.162), channel_id=1, replica_groups=mesh['rep'=16,'mp'=32] {'rep'}, dimensions={0}, use_global_device_ids=true | all-gather | bytes 348160 | tf_op jit(solution)/shard_map/all_gather | solution.py:125
  (84 shorter events, 15.7 us)
Async XLA Ops:
  7.2 26.5 %copy-start = (bf16[1024,256]{1,0:T(8,128)(2,1)S(1)}, bf16[1024,256]{1,0:T(8,128)(2,1)}, u32[]{:S(2)}) copy-start(bf16[1024,256]{1,0:T(8,128)(2,1)} %param.26) | copy-start | bytes 1572868
  7.2 25.4 %copy-start.13 = (bf16[1024]{0:T(1024)(128)(2,1)S(1)}, bf16[1024]{0:T(1024)(128)(2,1)}, u32[]{:S(2)}) copy-start(bf16[1024]{0:T(1024)(128)(2,1)} %param.25) | copy-start | bytes 6148
  7.2 25.4 %copy-start.15 = (bf16[256]{0:T(256)(128)(2,1)S(1)}, bf16[256]{0:T(256)(128)(2,1)}, u32[]{:S(2)}) copy-start(bf16[256]{0:T(256)(128)(2,1)} %param.27) | copy-start | bytes 1540
  7.2 25.4 %copy-start.11 = (bf16[128,13]{0,1:T(8,128)(2,1)S(1)}, bf16[128,13]{0,1:T(8,128)(2,1)}, u32[]{:S(2)}) copy-start(bf16[128,13]{0,1:T(8,128)(2,1)} %param.15) | copy-start | bytes 9988
  7.2 25.4 %copy-start.10 = (bf16[13,1024]{1,0:T(8,128)(2,1)S(1)}, bf16[13,1024]{1,0:T(8,128)(2,1)}, u32[]{:S(2)}) copy-start(bf16[13,1024]{1,0:T(8,128)(2,1)} %param.24) | copy-start | bytes 79876
  7.2 26.5 %copy-start.7 = (bf16[128,256]{1,0:T(8,128)(2,1)S(1)}, bf16[128,256]{1,0:T(8,128)(2,1)}, u32[]{:S(2)}) copy-start(bf16[128,256]{1,0:T(8,128)(2,1)} %param.29) | copy-start | bytes 196612
  7.2 1416.3 %all-gather.2.cloned.1.call-start = ((), (), s32[]{:S(2)}) async-start(), calls=%async_computation.3 | async-start | bytes 10506240 | tf_op jit(solution)/shard_map/all_gather | solution.py:56
  14.2 1409.4 %all-to-all-start = ((bf16[32,64,128]{2,1,0:T(8,128)(2,1)}), bf16[32,64,128]{2,1,0:T(8,128)(2,1)S(1)}, u32[]{:S(2)}, u32[]{:S(2)}) async-start(bf16[32,64,128]{2,1,0:T(8,128)(2,1)} %bitcast.68), calls=%async_computation | async-start | bytes 1048576 | tf_op jit(solution)/shard_map/all_to_all | solution.py:59
  32.5 1722.4 %reduce-scatter.3.cloned.1.call-start = ((), (), s32[]{:S(2)}) async-start(), calls=%async_computation.4 | async-start | bytes 11141120 | tf_op jit(solution)/shard_map/reduce_scatter | solution.py:118
  1423.6 1.6 slice-start.3
  1430.1 3.9 copy-start.8
  1430.1 4.0 copy-start.1
  1434.1 11.0 slice-start
  1434.1 11.0 slice-start.1
  1437.6 4.0 copy-start.4
  1437.6 4.2 copy-start.3
  1437.6 7.5 slice-start.2
  1459.8 4.8 copy-start.2
  1487.7 269.5 %copy-start.9 = (bf16[256,256]{1,0:T(8,128)(2,1)S(1)}, bf16[256,256]{1,0:T(8,128)(2,1)}, u32[]{:S(2)}) copy-start(bf16[256,256]{1,0:T(8,128)(2,1)} %param.21) | copy-start | bytes 393220
  1487.7 269.5 %copy-start.17 = (f32[128,256]{1,0:T(8,128)S(1)}, f32[128,256]{1,0:T(8,128)}, u32[]{:S(2)}) copy-start(f32[128,256]{1,0:T(8,128)} %get-tuple-element.91) | copy-start | bytes 393220
  1487.7 269.8 %copy-start.14 = (f32[256]{0:T(256)S(1)}, f32[256]{0:T(256)}, u32[]{:S(2)}) copy-start(f32[256]{0:T(256)} %get-tuple-element.85) | copy-start | bytes 3076
  1487.7 269.8 %copy-start.6 = (f32[128,1024]{1,0:T(8,128)S(1)}, f32[128,1024]{1,0:T(8,128)}, u32[]{:S(2)}) copy-start(f32[128,1024]{1,0:T(8,128)} %copy-done.5) | copy-start | bytes 1572868
  1487.7 270.1 %copy-start.12 = (bf16[128,13]{0,1:T(8,128)(2,1)S(1)}, bf16[128,13]{0,1:T(8,128)(2,1)}, u32[]{:S(2)}) copy-start(bf16[128,13]{0,1:T(8,128)(2,1)} %param.15) | copy-start | bytes 9988
  1487.7 385.2 %reduce-scatter.5.cloned.1.call-start = ((), (), s32[]{:S(2)}) async-start(), calls=%async_computation.5 | async-start | bytes 1351680 | tf_op jit(solution)/shard_map/reduce_scatter | solution.py:121
  (2 other events, 1.5 us)
Sparse Core Ops, SparseCore 0:
  11.9 1411.6 all-gather.1
  1487.8 267.0 reduce-scatter.2
  1759.3 113.5 reduce-scatter.4
where the time goes:
time: 1930 us
  waiting for transfers between devices  1650 us (85%)
  blocking collectives  158 us (8%)
  local copies, waits for them, and re-layouts  50.2 us (3%)
  matrix products  26 us (1%)
    all_gather x1, waiting for transfers between devices, local(): packed = lax.all_gather(packed, ('mp', 'rep'), axis=0, tiled=True)  1390 us
    reduce_scatter x1, waiting for transfers between devices, local(): lax.psum_scatter(grads.reshape(replicas * tables * share, columns), 'rep'...  266 us
    psum x1, blocking collectives, local(): lax.psum((grad_wf, grad_bf, grad_ws, grad_bs, grad_vb, grad_ub, grad_bb),...  114 us
    all_gather x1, blocking collectives, local(): grads = lax.all_gather(grads, 'rep', axis=0, tiled=True)  44.4 us
  transfers between devices with their start and end apart: 4, of which 3 were waited for; matrix products, arithmetic and copies ran while one was open for 0% of the time, Pallas kernels for 0%

commit v1 on v0

--- a/solution.py
+++ b/solution.py
@@ -122,7 +122,10 @@
         grads.astype(jnp.float32) * grad_scale, "mp", scatter_dimension=0, tiled=True
     )
     grads = lax.optimization_barrier(grads).astype(jnp.bfloat16)
-    grads = lax.all_gather(grads, "rep", axis=0, tiled=True)
+    size = lax.axis_size("rep")
+    shards = jnp.stack([grads for _ in range(size)])
+    shards = lax.all_to_all(shards, "rep", split_axis=0, concat_axis=0)
+    grads = jnp.concatenate(shards, axis=0)
     d_bottom = cot_low * (lift_bottom + 1.0) + contract_cols(d_low, v_bot)
     grad_vb = grad_scale * contract_rows(bottom, d_low)
     grad_ub = grad_scale * contract_rows(low_rank, d_bottom_round)

time: 1930 us -> 2000 us (1.036)
  the two profiles are of different devices: /device:TPU:8 before, /device:TPU:1 now
where the time goes in v1:
time: 2000 us
  waiting for transfers between devices  1770 us (88%)
  blocking collectives  114 us (6%)
  local copies, waits for them, and re-layouts  50.7 us (3%)
  matrix products  26 us (1%)
  starting transfers between devices  23.9 us (1%)
    all_gather x1, waiting for transfers between devices, local(): packed = lax.all_gather(packed, ('mp', 'rep'), axis=0, tiled=True)  1410 us
    reduce_scatter x1, waiting for transfers between devices, local(): lax.psum_scatter(grads.reshape(replicas * tables * share, columns), 'rep'...  241 us
    psum x1, blocking collectives, local(): lax.psum((grad_wf, grad_bf, grad_ws, grad_bs, grad_vb, grad_ub, grad_bb),...  114 us
    reduce_scatter x1, waiting for transfers between devices, local(): lax.psum_scatter(grads.astype(jnp.float32) * grad_scale, 'mp', scatter_di...  113 us
  transfers between devices with their start and end apart: 5, of which 3 were waited for; matrix products, arithmetic and copies ran while one was open for 0% of the time, Pallas kernels for 0%

profile of v1, /device:TPU:1, one launch (start us, length us, event | category | flops | bytes accessed | tf_op | source)
XLA Modules:
  0.0 2003.0 jit_solution(8442828560587823694)
XLA Ops:
  14.2 19.4 all-to-all-start
  34.8 1.5 fusion.23
  36.3 1414.0 %all-gather.2.cloned.1.call-done = bf16[8192,640]{1,0:T(8,128)(2,1)} async-done(((bf16[16,640]{1,0:T(8,128)(2,1)}), bf16[8192,640]{1,0:T(8,128)(2,1)}) %all-gather.2.cloned.1.call-update) | async-done | bytes 10485776 | tf_op jit(solution)/shard_map/all_gather | solution.py:56
  1450.3 1.6 slice-done.3
  1451.9 2.0 convolution_convert_fusion.2
  1453.9 2.9 copy.77
  1456.8 3.8 fusion.9
  1460.9 3.4 convolution_convert_fusion
  1464.3 4.0 fusion.5
  1468.5 3.3 convolution_convert_fusion.1
  1473.2 3.0 fusion.3
  1476.3 1.6 fusion.1
  1478.3 1.8 copy.79
  1480.0 2.1 copy.82
  1482.3 4.2 copy.83
  1486.5 4.8 copy.81
  1491.4 2.5 copy.80
  1493.9 1.7 broadcast_in_dim.18
  1495.6 18.8 concatenate.14
  1514.6 241.1 %reduce-scatter.3.cloned.1.call-done = bf16[512,640]{1,0:T(8,128)(2,1)} async-done(((bf16[8192,640]{1,0:T(8,128)(2,1)}), bf16[512,640]{1,0:T(8,128)(2,1)}) %reduce-scatter.3.cloned.1.call-update) | async-done | bytes 655376 | tf_op jit(solution)/shard_map/reduce_scatter | solution.py:118
  1755.7 2.3 convert_multiply_fusion.3
  1759.4 113.2 %reduce-scatter.5.cloned.1.call-done = f32[16,640]{1,0:T(8,128)} async-done(((f32[512,640]{1,0:T(8,128)}), f32[16,640]{1,0:T(8,128)}) %reduce-scatter.5.cloned.1.call-update) | async-done | bytes 40976 | tf_op jit(solution)/shard_map/reduce_scatter | solution.py:121
  1874.2 4.4 all-to-all-start.1
  1879.5 114.0 %all-reduce.2 = (bf16[256,256]{1,0:T(8,128)(2,1)}, bf16[256,256]{1,0:T(8,128)(2,1)}, bf16[256]{0:T(256)(128)(2,1)}, bf16[13,1024]{1,0:T(8,128)(2,1)}, bf16[1024]...) all-reduce(f32[256,256]{1,0:T(8,128)S(1)} %convolution_multiply_fus, ...), channel_id=1, replica_groups=mesh['rep'=16,'mp'=32] {'rep','mp'}, use_global_device_ids=true, to_apply=%region_3.4 | all-reduce | flops 408064 | bytes 2448384 | tf_op jit(solution)/shard_map/psum | solution.py:141
  (86 shorter events, 17.3 us)
Async XLA Ops:
  7.2 27.6 %copy-start = (bf16[1024,256]{1,0:T(8,128)(2,1)S(1)}, bf16[1024,256]{1,0:T(8,128)(2,1)}, u32[]{:S(2)}) copy-start(bf16[1024,256]{1,0:T(8,128)(2,1)} %param.26) | copy-start | bytes 1572868
  7.2 26.4 %copy-start.13 = (bf16[1024]{0:T(1024)(128)(2,1)S(1)}, bf16[1024]{0:T(1024)(128)(2,1)}, u32[]{:S(2)}) copy-start(bf16[1024]{0:T(1024)(128)(2,1)} %param.25) | copy-start | bytes 6148
  7.2 26.4 %copy-start.15 = (bf16[256]{0:T(256)(128)(2,1)S(1)}, bf16[256]{0:T(256)(128)(2,1)}, u32[]{:S(2)}) copy-start(bf16[256]{0:T(256)(128)(2,1)} %param.27) | copy-start | bytes 1540
  7.2 26.4 %copy-start.11 = (bf16[128,13]{0,1:T(8,128)(2,1)S(1)}, bf16[128,13]{0,1:T(8,128)(2,1)}, u32[]{:S(2)}) copy-start(bf16[128,13]{0,1:T(8,128)(2,1)} %param.15) | copy-start | bytes 9988
  7.2 26.4 %copy-start.10 = (bf16[13,1024]{1,0:T(8,128)(2,1)S(1)}, bf16[13,1024]{1,0:T(8,128)(2,1)}, u32[]{:S(2)}) copy-start(bf16[13,1024]{1,0:T(8,128)(2,1)} %param.24) | copy-start | bytes 79876
  7.2 27.6 %copy-start.7 = (bf16[128,256]{1,0:T(8,128)(2,1)S(1)}, bf16[128,256]{1,0:T(8,128)(2,1)}, u32[]{:S(2)}) copy-start(bf16[128,256]{1,0:T(8,128)(2,1)} %param.29) | copy-start | bytes 196612
  7.2 1443.1 %all-gather.2.cloned.1.call-start = ((), (), s32[]{:S(2)}) async-start(), calls=%async_computation.4 | async-start | bytes 10506240 | tf_op jit(solution)/shard_map/all_gather | solution.py:56
  14.2 1436.1 %all-to-all-start = ((bf16[32,64,128]{2,1,0:T(8,128)(2,1)}), bf16[32,64,128]{2,1,0:T(8,128)(2,1)S(1)}, u32[]{:S(2)}, u32[]{:S(2)}) async-start(bf16[32,64,128]{2,1,0:T(8,128)(2,1)} %bitcast.69), calls=%async_computation | async-start | bytes 1048576 | tf_op jit(solution)/shard_map/all_to_all | solution.py:59
  33.6 1722.1 %reduce-scatter.3.cloned.1.call-start = ((), (), s32[]{:S(2)}) async-start(), calls=%async_computation.5 | async-start | bytes 11141120 | tf_op jit(solution)/shard_map/reduce_scatter | solution.py:118
  1456.8 4.0 copy-start.1
  1460.8 11.0 slice-start
  1460.9 11.0 slice-start.1
  1464.3 4.0 copy-start.4
  1464.3 4.2 copy-start.3
  1464.3 7.5 slice-start.2
  1486.5 4.8 copy-start.2
  1514.4 243.5 %copy-start.16 = (bf16[256]{0:T(256)(128)(2,1)S(1)}, bf16[256]{0:T(256)(128)(2,1)}, u32[]{:S(2)}) copy-start(bf16[256]{0:T(256)(128)(2,1)} %param.23) | copy-start | bytes 1540
  1514.4 244.3 %copy-start.9 = (bf16[256,256]{1,0:T(8,128)(2,1)S(1)}, bf16[256,256]{1,0:T(8,128)(2,1)}, u32[]{:S(2)}) copy-start(bf16[256,256]{1,0:T(8,128)(2,1)} %param.21) | copy-start | bytes 393220
  1514.4 244.3 %copy-start.17 = (f32[128,256]{1,0:T(8,128)S(1)}, f32[128,256]{1,0:T(8,128)}, u32[]{:S(2)}) copy-start(f32[128,256]{1,0:T(8,128)} %get-tuple-element.91) | copy-start | bytes 393220
  1514.5 244.5 %copy-start.14 = (f32[256]{0:T(256)S(1)}, f32[256]{0:T(256)}, u32[]{:S(2)}) copy-start(f32[256]{0:T(256)} %get-tuple-element.85) | copy-start | bytes 3076
  1514.5 244.6 %copy-start.6 = (f32[128,1024]{1,0:T(8,128)S(1)}, f32[128,1024]{1,0:T(8,128)}, u32[]{:S(2)}) copy-start(f32[128,1024]{1,0:T(8,128)} %copy-done.5) | copy-start | bytes 1572868
  1514.5 364.1 %copy-start.12 = (bf16[128,13]{0,1:T(8,128)(2,1)S(1)}, bf16[128,13]{0,1:T(8,128)(2,1)}, u32[]{:S(2)}) copy-start(bf16[128,13]{0,1:T(8,128)(2,1)} %param.15) | copy-start | bytes 9988
  1514.5 358.1 %reduce-scatter.5.cloned.1.call-start = ((), (), s32[]{:S(2)}) async-start(), calls=%async_computation.6 | async-start | bytes 1351680 | tf_op jit(solution)/shard_map/reduce_scatter | solution.py:121
  1874.2 119.4 %all-to-all-start.1 = ((bf16[16,16,640]{2,1,0:T(8,128)(2,1)}), bf16[16,16,640]{2,1,0:T(8,128)(2,1)S(1)}, u32[]{:S(2)}, u32[]{:S(2)}) async-start(bf16[16,16,640]{2,1,0:T(8,128)(2,1)} %stack.2), calls=%async_computation.3 | async-start | bytes 655360 | tf_op jit(solution)/shard_map/all_to_all | solution.py:127
  (3 other events, 6.3 us)
Sparse Core Ops, SparseCore 0:
  11.9 1438.3 all-gather.1
  1514.6 241.0 reduce-scatter.2
  1760.1 112.4 reduce-scatter.4
